TPU v7x, 32 devices: a whole 2x2x4 slice. The times are simulated.
32 devices in a mesh: row: 2 (over y), col: 4 (over x, core), tm: 4 (over z).
Axes of the slice: x: 2, y: 2, z: 4, core: 2. Of those that a mesh axis runs over, the one named last changes fastest.
Arguments:
- filled_orbitals: bfloat16 [4, 1024, 1024], P('col', 'row', 'tm'), may hold values from -0.1875 to 0.1875
- empty_orbitals: bfloat16 [4, 1024, 3072], P('col', 'row', 'tm'), may hold values from -0.109375 to 0.109375
- filled_depth: bfloat16 [1024], P('tm'), may hold values from 0.019897461 to 2
- empty_depth: bfloat16 [3072], P('tm'), may hold values from 0.019897461 to 2
- time_points: float32 [4], P('tm'), may hold values from 0.05 to 8
- cosine_weights: float32 [4, 4], replicated, may hold values from -3 to 3
Outputs:
- polar_freq: float32 [4, 4, 1024, 4096], P(None, None, ('row', 'tm'), 'col')
All inputs are finite; a program needn't handle non-finite values.
Results may differ from a plain program's by a relative error of at most 0.0033.
Values may be sent and summed in bfloat16 or wider, within the bound.
No kernel may reach another device: no remote copies, remote signals or barrier semaphores. Data moves between devices by JAX's collectives and lax.ppermute only.
A program may use at most 128 MiB of HBM per device.

v0:
```python
import jax
import jax.numpy as jnp
from jax import lax
from jax.sharding import PartitionSpec as P


def tile_product(left_points, right_points, depths, tau_value):
    band_count = left_points.shape[-1]
    weight_row = jnp.exp(-depths.astype(jnp.float32) * tau_value)
    scaled = (
        right_points.reshape(-1, band_count).astype(jnp.float32) * weight_row[None, :]
    ).astype(jnp.bfloat16)
    return lax.dot_general(
        left_points.reshape(-1, band_count),
        scaled,
        (((1,), (1,)), ((), ())),
        preferred_element_type=jnp.float32,
    )


def on_device(
    filled_orbitals, empty_orbitals, filled_depth, empty_depth, time_points, cosine_weights
):
    tau_value = time_points[0]
    filled_bands, empty_bands, filled_all, empty_all = (
        lax.all_gather(filled_orbitals, "tm", axis=2, tiled=True),
        lax.all_gather(empty_orbitals, "tm", axis=2, tiled=True),
        lax.all_gather(filled_depth, "tm", axis=0, tiled=True),
        lax.all_gather(empty_depth, "tm", axis=0, tiled=True),
    )
    filled_rows, empty_rows = (
        lax.all_gather(filled_bands, "col", axis=0, tiled=True),
        lax.all_gather(empty_bands, "col", axis=0, tiled=True),
    )
    column_filled, column_empty = lax.all_gather(
        (filled_bands, empty_bands), "row", axis=1, tiled=True
    )
    green_filled = tile_product(filled_rows, column_filled, filled_all, tau_value)
    green_empty = tile_product(empty_rows, column_empty, empty_all, tau_value)
    polar_time = (
        (-(green_filled * green_empty))
        .astype(jnp.bfloat16)
        .reshape(filled_rows.shape[0], filled_rows.shape[1], -1)
    )
    return jnp.einsum(
        "ft,tabc->fabc",
        cosine_weights,
        lax.all_to_all(polar_time[None], "tm", split_axis=2, concat_axis=0, tiled=True).astype(
            jnp.float32
        ),
        precision=lax.Precision.HIGHEST,
    )


def solution(mesh):
    in_specs = (P("col", "row", "tm"), P("col", "row", "tm"), P("tm"), P("tm"), P("tm"), P())
    out_specs = P(None, None, ("row", "tm"), "col")
    return jax.shard_map(
        on_device, mesh=mesh, in_specs=in_specs, out_specs=out_specs, check_vma=False
    )
```

profile of v0, /device:TPU:0, one launch (start us, length us, event | category | flops | bytes accessed | tf_op | source)
XLA Modules:
  0.0 491.7 jit_solution(13205183618008928850)
XLA Ops:
  6.5 0.0 copy-start
  6.5 0.0 all-gather.15.cloned.1.call-start
  6.5 0.7 all-gather.15.cloned.1.call-update
  7.3 0.0 all-gather.9.cloned.1.call-start
  7.3 0.7 all-gather.9.cloned.1.call-update
  8.0 0.0 all-gather.17.cloned.1.call-start
  8.1 67.0 %all-gather.15.cloned.1.call-done = bf16[1,512,3072]{2,1,0:T(8,128)(2,1)} async-done(((bf16[1,512,768]{2,1,0:T(8,128)(2,1)}), bf16[1,512,3072]{2,1,0:T(8,128)(2,1)}) %all-gather.15.cloned.1.call-update) | async-done | bytes 3145744 | tf_op jit(solution)/shard_map/all_gather | solution.py:27
  75.1 0.0 copy-start.1
  75.1 0.0 all-gather.17.cloned.1.call-update
  75.1 0.0 all-gather.19.cloned.1.call-start
  75.2 0.5 all-gather.19.cloned.1.call-update
  75.7 0.0 all-gather.11.cloned.1.call-start
  75.8 29.5 %all-gather.9.cloned.1.call-done = bf16[1,512,1024]{2,1,0:T(8,128)(2,1)} async-done(((bf16[1,512,256]{2,1,0:T(8,128)(2,1)}), bf16[1,512,1024]{2,1,0:T(8,128)(2,1)}) %all-gather.9.cloned.1.call-update) | async-done | bytes 1048592 | tf_op jit(solution)/shard_map/all_gather | solution.py:26
  105.3 0.0 all-gather.11.cloned.1.call-update
  105.3 0.0 all-gather.13.cloned.1.call-start
  105.3 0.5 all-gather.13.cloned.1.call-update
  106.5 0.0 copy-done.1
  106.5 0.0 copy-done.2
  106.6 10.1 %all-gather = bf16[4,1,256]{2,1,0:T(2,128)(2,1)S(1)} all-gather(bf16[1,1,256]{2,1,0:T(2,128)(2,1)S(1)} %reshape.26), channel_id=1, replica_groups=mesh['row'=2,'col'=4,'tm'=4] {'tm'}, dimensions={0}, use_global_device_ids=true | all-gather | bytes 2560 | tf_op jit(solution)/shard_map/all_gather | solution.py:28
  116.7 13.1 %all-gather.1 = bf16[4,1,768]{2,1,0:T(2,128)(2,1)S(1)} all-gather(bf16[1,1,768]{2,1,0:T(2,128)(2,1)S(1)} %reshape.28), channel_id=1, replica_groups=mesh['row'=2,'col'=4,'tm'=4] {'tm'}, dimensions={0}, use_global_device_ids=true | all-gather | bytes 7680 | tf_op jit(solution)/shard_map/all_gather | solution.py:29
  129.8 55.7 %all-gather.17.cloned.1.call-done = bf16[1,1024,3072]{2,1,0:T(8,128)(2,1)} async-done(((bf16[1,512,3072]{2,1,0:T(8,128)(2,1)}), bf16[1,1024,3072]{2,1,0:T(8,128)(2,1)}) %all-gather.17.cloned.1.call-update) | async-done | bytes 6291472 | tf_op jit(solution)/shard_map/all_gather | solution.py:35
  185.5 83.5 %all-gather.19.cloned.1.call-done = bf16[4,512,3072]{2,1,0:T(8,128)(2,1)} async-done(((bf16[1,512,3072]{2,1,0:T(8,128)(2,1)}), bf16[4,512,3072]{2,1,0:T(8,128)(2,1)}) %all-gather.19.cloned.1.call-update) | async-done | bytes 12582928 | tf_op jit(solution)/shard_map/all_gather | solution.py:33
  269.0 18.9 %fusion.1 = f32[1024,2048]{1,0:T(8,128)} fusion(bf16[2048,3072]{1,0:T(8,128)(2,1)} %bitcast.35, bf16[1,1024,3072]{2,1,0:T(8,128)(2,1)} %all-gather.17.cloned.1.call-done, f32[3072]{0:T(1024)S(1)} %bitcast.33), kind=kOutput, calls=%fused_computation.3 | convolution fusion | flops 12894339072 | bytes 27275264 | tf_op jit(solution)/shard_map/dot_general | solution.py:13
  287.9 15.6 %all-gather.11.cloned.1.call-done = bf16[1,1024,1024]{2,1,0:T(8,128)(2,1)} async-done(((bf16[1,512,1024]{2,1,0:T(8,128)(2,1)}), bf16[1,1024,1024]{2,1,0:T(8,128)(2,1)}) %all-gather.11.cloned.1.call-update) | async-done | bytes 2097168 | tf_op jit(solution)/shard_map/all_gather | solution.py:35
  303.5 35.9 %all-gather.13.cloned.1.call-done = bf16[4,512,1024]{2,1,0:T(8,128)(2,1)} async-done(((bf16[1,512,1024]{2,1,0:T(8,128)(2,1)}), bf16[4,512,1024]{2,1,0:T(8,128)(2,1)}) %all-gather.13.cloned.1.call-update) | async-done | bytes 4194320 | tf_op jit(solution)/shard_map/all_gather | solution.py:32
  339.4 11.8 %fusion.6 = bf16[2048,1024]{0,1:T(8,128)(2,1)} fusion(f32[1024,2048]{1,0:T(8,128)} %fusion.1, bf16[2048,1024]{1,0:T(8,128)(2,1)} %bitcast.36, bf16[1,1024,1024]{2,1,0:T(8,128)(2,1)} %all-gather.11.cloned.1.call-done, f32[1024]{0:T(1024)S(1)} %bitcast.34), kind=kOutput, calls=%fused_computation.9 | convolution fusion | flops 4304404480 | bytes 18878464 | tf_op jit(solution)/shard_map/dot_general | solution.py:13
  351.2 7.8 %broadcast_in_dim_reshape.3 = bf16[1,4,512,1024]{2,1,3,0:T(4,128)(2,1)} reshape(bf16[2048,1024]{0,1:T(8,128)(2,1)} %fusion.6) | data formatting | bytes 8388608 | tf_op jit(solution)/shard_map/broadcast_in_dim;reshape | solution.py:48
  359.0 10.0 %copy.11 = bf16[1,4,512,1024]{3,1,0,2:T(4,128)(2,1)} copy(bf16[1,4,512,1024]{2,1,3,0:T(4,128)(2,1)} %broadcast_in_dim_reshape.3) | data formatting | bytes 8388608 | tf_op jit(solution)/shard_map/broadcast_in_dim;reshape | solution.py:48
  369.0 98.1 %all_to_all.18 = bf16[1,4,512,1024]{3,1,0,2:T(4,128)(2,1)S(1)} all-to-all(bf16[1,4,512,1024]{3,1,0,2:T(4,128)(2,1)} %copy.11), channel_id=1, replica_groups=mesh['row'=2,'col'=4,'tm'=4] {'tm'}, dimensions={2} | all-to-all | bytes 8388608 | tf_op jit(solution)/shard_map/all_to_all | solution.py:48
  467.2 0.0 copy-done
  467.2 9.4 %convolution_bitcast_fusion = f32[4,4,128,1024]{3,0,2,1:T(4,128)S(1)} fusion(bf16[1,4,4,128,1024]{4,1,3,2,0:T(4,128)(2,1)S(1)} %bitcast.32, f32[4,4]{1,0:T(4,128)S(1)} %copy-done), kind=kOutput, calls=%fused_computation.5 | convolution fusion | flops 100663296 | bytes 12582976 | tf_op jit(solution)/shard_map/ft,tabc->fabc/dot_general | solution.py:45
  476.6 8.3 %copy.14 = f32[4,4,128,1024]{3,2,1,0:T(8,128)} copy(f32[4,4,128,1024]{3,0,2,1:T(4,128)S(1)} %convolution_bitcast_fusion) | data formatting | bytes 16777216 | tf_op jit(solution)/shard_map/ft,tabc->fabc/dot_general | solution.py:45
  (5 shorter events, 0.1 us)
Async XLA Ops:
  6.5 460.6 %copy-start = (f32[4,4]{1,0:T(4,128)S(1)}, f32[4,4]{1,0:T(4,128)}, u32[]{:S(2)}) copy-start(f32[4,4]{1,0:T(4,128)} %param.11) | copy-start | bytes 196
  6.5 68.6 %all-gather.15.cloned.1.call-start = ((), (), s32[]{:S(2)}) async-start(), calls=%async_computation.4 | async-start | bytes 3932160 | tf_op jit(solution)/shard_map/all_gather | solution.py:27
  7.3 98.0 %all-gather.9.cloned.1.call-start = ((), (), s32[]{:S(2)}) async-start(), calls=%async_computation.1 | async-start | bytes 1310720 | tf_op jit(solution)/shard_map/all_gather | solution.py:26
  8.0 177.5 %all-gather.17.cloned.1.call-start = ((), (), s32[]{:S(2)}) async-start(), calls=%async_computation.5 | async-start | bytes 9437184 | tf_op jit(solution)/shard_map/all_gather | solution.py:35
  75.1 31.4 %copy-start.1 = (bf16[768]{0:T(1024)(128)(2,1)S(1)}, bf16[768]{0:T(1024)(128)(2,1)}, u32[]{:S(2)}) copy-start(bf16[768]{0:T(1024)(128)(2,1)} %param.9) | copy-start | bytes 4612
  75.1 31.4 %copy-start.2 = (bf16[256]{0:T(256)(128)(2,1)S(1)}, bf16[256]{0:T(256)(128)(2,1)}, u32[]{:S(2)}) copy-start(bf16[256]{0:T(256)(128)(2,1)} %param.8) | copy-start | bytes 1540
  75.1 193.9 %all-gather.19.cloned.1.call-start = ((), (), s32[]{:S(2)}) async-start(), calls=%async_computation.6 | async-start | bytes 15728640 | tf_op jit(solution)/shard_map/all_gather | solution.py:33
  75.7 227.8 %all-gather.11.cloned.1.call-start = ((), (), s32[]{:S(2)}) async-start(), calls=%async_computation.2 | async-start | bytes 3145728 | tf_op jit(solution)/shard_map/all_gather | solution.py:35
  105.3 234.2 %all-gather.13.cloned.1.call-start = ((), (), s32[]{:S(2)}) async-start(), calls=%async_computation.3 | async-start | bytes 5242880 | tf_op jit(solution)/shard_map/all_gather | solution.py:32
Sparse Core Ops, SparseCore 0:
  8.9 66.1 all-gather.14
  76.7 28.5 all-gather.8
  106.8 78.6 all-gather.16
  186.9 82.0 all-gather.18
  270.4 33.0 all-gather.10
  305.0 34.4 all-gather.12
where the time goes:
time: 492 us
  waiting for transfers between devices  290 us (59%)
  blocking collectives  121 us (25%)
  matrix products  40.1 us (8%)
  local copies, waits for them, and re-layouts  26.1 us (5%)
  between operations  14.2 us (3%)
    all_to_all x1, blocking collectives, on_device(): lax.all_to_all(polar_time[None], 'tm', split_axis=2, concat_axis=0, tiled...  98.1 us
    all_gather x1, waiting for transfers between devices, on_device(): lax.all_gather(empty_bands, 'col', axis=0, tiled=True)  83.5 us
    all_gather x2, waiting for transfers between devices, on_device(): lax.all_gather((filled_bands, empty_bands), 'row', axis=1, tiled=True)  71.3 us
    all_gather x1, waiting for transfers between devices, on_device(): lax.all_gather(empty_orbitals, 'tm', axis=2, tiled=True)  67 us
    all_gather x1, waiting for transfers between devices, on_device(): lax.all_gather(filled_bands, 'col', axis=0, tiled=True)  35.9 us
    dot_general x2, matrix products, tile_product(): lax.dot_general(left_points.reshape(-1, band_count), scaled, (((1,), (1,)...  30.6 us
    all_gather x1, waiting for transfers between devices, on_device(): lax.all_gather(filled_orbitals, 'tm', axis=2, tiled=True)  29.5 us
    another operation x2, local copies, waits for them, and re-layouts, on_device(): polar_time[None]  17.8 us
  transfers between devices with their start and end apart: 6, of which 6 were waited for; matrix products, arithmetic and copies ran while one was open for 4% of the time, Pallas kernels for 0%

commit v1 on v0

--- a/solution.py
+++ b/solution.py
@@ -2,6 +2,26 @@
 import jax.numpy as jnp
 from jax import lax
 from jax.sharding import PartitionSpec as P
+
+
+def store_threads_on_mesh(xs, mesh_dim, array_dim):
+    prior, all_values, mid_arr = (
+        lax.axis_size(mesh_dim),
+        lax.axis_index(mesh_dim),
+        xs.shape[array_dim],
+    )
+    ledger = [i * prior if to_i == array_dim else i for to_i, i in enumerate(xs.shape)]
+    reached = lax.dynamic_update_slice_in_dim(
+        jnp.zeros(ledger, xs.dtype), xs, all_values * mid_arr, axis=array_dim
+    )
+    w = 1
+    while w < prior:
+        xs = lax.ppermute(xs, mesh_dim, [(to_i, (to_i + 1) % prior) for to_i in range(prior)])
+        reached = lax.dynamic_update_slice_in_dim(
+            reached, xs, (all_values - w) % prior * mid_arr, axis=array_dim
+        )
+        w += 1
+    return reached
 
 
 def tile_product(left_points, right_points, depths, tau_value):
@@ -29,7 +49,7 @@
         lax.all_gather(empty_depth, "tm", axis=0, tiled=True),
     )
     filled_rows, empty_rows = (
-        lax.all_gather(filled_bands, "col", axis=0, tiled=True),
+        store_threads_on_mesh(filled_bands, "col", 0),
         lax.all_gather(empty_bands, "col", axis=0, tiled=True),
     )
     column_filled, column_empty = lax.all_gather(

time: 492 us -> 438 us (0.89)
  waiting for transfers between devices: 290 us -> 245 us
  local copies, waits for them, and re-layouts: 26.1 us -> 19.5 us
    all_gather x2, waiting for transfers between devices: 71.3 us -> 34.7 us  [on_device(): lax.all_gather((filled_bands, empty_bands), 'row', axis=1, tiled=True)]
    all_gather x1 -> x0, waiting for transfers between devices: 35.9 us -> none  [on_device(): lax.all_gather(filled_bands, 'col', axis=0, tiled=True)]
    ppermute x0 -> x3, waiting for transfers between devices: none -> 28.7 us  [store_threads_on_mesh(): lax.ppermute(xs, mesh_dim, [(to_i, (to_i + 1) % prior) for to_i in range(...]
    another operation x2 -> x1, local copies, waits for them, and re-layouts: 17.8 us -> 3.24 us  [on_device(): polar_time[None]]
    dynamic_update_slice x0 -> x4, local copies, waits for them, and re-layouts: none -> 5.43 us  [the longest x3 4.38 us: store_threads_on_mesh(): lax.dynamic_update_slice_in_dim(reached, xs, (all_values - w) % prior * m...]
  transfers between devices with their start and end apart: 6 -> 8, of which waited for: 6 -> 7; matrix products, arithmetic and copies ran while one was open for 4% -> 6% of each run, Pallas kernels for 0% -> 0%
where the time goes in v1:
time: 438 us
  waiting for transfers between devices  245 us (56%)
  blocking collectives  121 us (28%)
  matrix products  38.6 us (9%)
  local copies, waits for them, and re-layouts  19.5 us (4%)
  between operations  13.9 us (3%)
    all_to_all x1, blocking collectives, on_device(): lax.all_to_all(polar_time[None], 'tm', split_axis=2, concat_axis=0, tiled...  97.4 us
    all_gather x1, waiting for transfers between devices, on_device(): lax.all_gather(empty_bands, 'col', axis=0, tiled=True)  83.5 us
    all_gather x1, waiting for transfers between devices, on_device(): lax.all_gather(empty_orbitals, 'tm', axis=2, tiled=True)  67 us
    all_gather x2, waiting for transfers between devices, on_device(): lax.all_gather((filled_bands, empty_bands), 'row', axis=1, tiled=True)  34.7 us
    all_gather x1, waiting for transfers between devices, on_device(): lax.all_gather(filled_orbitals, 'tm', axis=2, tiled=True)  29.5 us
    dot_general x2, matrix products, tile_product(): lax.dot_general(left_points.reshape(-1, band_count), scaled, (((1,), (1,)...  29.2 us
    ppermute x3, waiting for transfers between devices, store_threads_on_mesh(): lax.ppermute(xs, mesh_dim, [(to_i, (to_i + 1) % prior) for to_i in range(...  28.7 us
    all_gather x1, blocking collectives, on_device(): lax.all_gather(empty_depth, 'tm', axis=0, tiled=True)  13.1 us
  transfers between devices with their start and end apart: 8, of which 7 were waited for; matrix products, arithmetic and copies ran while one was open for 6% of the time, Pallas kernels for 0%

profile of v1, /device:TPU:0, one launch (start us, length us, event | category | flops | bytes accessed | tf_op | source)
XLA Modules:
  0.0 438.3 jit_solution(1217180541809440306)
XLA Ops:
  6.5 0.7 all-gather.12.cloned.1.call-update
  7.3 0.0 all-gather.8.cloned.1.call-start
  7.3 0.7 all-gather.8.cloned.1.call-update
  8.0 0.0 all-gather.14.cloned.1.call-start
  8.1 67.0 %all-gather.12.cloned.1.call-done = bf16[1,512,3072]{2,1,0:T(8,128)(2,1)} async-done(((bf16[1,512,768]{2,1,0:T(8,128)(2,1)}), bf16[1,512,3072]{2,1,0:T(8,128)(2,1)}) %all-gather.12.cloned.1.call-update) | async-done | bytes 3145744 | tf_op jit(solution)/shard_map/all_gather | solution.py:47
  75.1 0.0 all-gather.14.cloned.1.call-update
  75.1 0.0 all-gather.16.cloned.1.call-start
  75.2 0.5 all-gather.16.cloned.1.call-update
  75.7 0.0 all-gather.10.cloned.1.call-start
  75.8 29.5 %all-gather.8.cloned.1.call-done = bf16[1,512,1024]{2,1,0:T(8,128)(2,1)} async-done(((bf16[1,512,256]{2,1,0:T(8,128)(2,1)}), bf16[1,512,1024]{2,1,0:T(8,128)(2,1)}) %all-gather.8.cloned.1.call-update) | async-done | bytes 1048592 | tf_op jit(solution)/shard_map/all_gather | solution.py:46
  105.3 0.0 collective-permute-start
  105.3 14.4 %collective-permute-done = bf16[1,512,1024]{2,1,0:T(8,128)(2,1)S(1)} collective-permute-done((bf16[1,512,1024]{2,1,0:T(8,128)(2,1)}, bf16[1,512,1024]{2,1,0:T(8,128)(2,1)S(1)}, u32[]{:S(2)}, u32[]{:S(2)}) %collective-permute-start) | collective-permute-done | bytes 1048608 | tf_op jit(solution)/shard_map/ppermute | solution.py:19
  119.7 0.0 collective-permute-start.1
  119.7 14.2 %collective-permute-done.1 = bf16[1,512,1024]{2,1,0:T(8,128)(2,1)S(1)} collective-permute-done((bf16[1,512,1024]{2,1,0:T(8,128)(2,1)S(1)}, bf16[1,512,1024]{2,1,0:T(8,128)(2,1)S(1)}, u32[]{:S(2)}, u32[]{:S(2)}) %collective-permute-start.1) | collective-permute-done | bytes 1048608 | tf_op jit(solution)/shard_map/ppermute | solution.py:19
  133.9 0.0 collective-permute-start.2
  134.6 10.1 %all-gather = bf16[4,1,256]{2,1,0:T(2,128)(2,1)S(1)} all-gather(bf16[1,1,256]{2,1,0:T(2,128)(2,1)S(1)} %reshape.26), channel_id=1, replica_groups=mesh['row'=2,'col'=4,'tm'=4] {'tm'}, dimensions={0}, use_global_device_ids=true | all-gather | bytes 2560 | tf_op jit(solution)/shard_map/all_gather | solution.py:48
  144.7 13.1 %all-gather.1 = bf16[4,1,768]{2,1,0:T(2,128)(2,1)S(1)} all-gather(bf16[1,1,768]{2,1,0:T(2,128)(2,1)S(1)} %reshape.28), channel_id=1, replica_groups=mesh['row'=2,'col'=4,'tm'=4] {'tm'}, dimensions={0}, use_global_device_ids=true | all-gather | bytes 7680 | tf_op jit(solution)/shard_map/all_gather | solution.py:49
  157.9 0.0 all-gather.10.cloned.1.call-update
  157.9 2.6 broadcast_in_dim.2
  160.5 1.0 constant_dynamic-update-slice_fusion.3
  161.6 1.1 constant_dynamic-update-slice_fusion.2
  162.6 1.0 constant_dynamic-update-slice_fusion.1
  163.7 2.3 constant_dynamic-update-slice_fusion
  166.0 19.6 %all-gather.14.cloned.1.call-done = bf16[1,1024,3072]{2,1,0:T(8,128)(2,1)} async-done(((bf16[1,512,3072]{2,1,0:T(8,128)(2,1)}), bf16[1,1024,3072]{2,1,0:T(8,128)(2,1)}) %all-gather.14.cloned.1.call-update) | async-done | bytes 6291472 | tf_op jit(solution)/shard_map/all_gather | solution.py:55
  185.5 83.5 %all-gather.16.cloned.1.call-done = bf16[4,512,3072]{2,1,0:T(8,128)(2,1)} async-done(((bf16[1,512,3072]{2,1,0:T(8,128)(2,1)}), bf16[4,512,3072]{2,1,0:T(8,128)(2,1)}) %all-gather.16.cloned.1.call-update) | async-done | bytes 12582928 | tf_op jit(solution)/shard_map/all_gather | solution.py:53
  269.0 19.4 %fusion.3 = f32[1024,2048]{0,1:T(8,128)} fusion(bf16[2048,3072]{1,0:T(8,128)(2,1)} %bitcast.39, bf16[1,1024,3072]{2,1,0:T(8,128)(2,1)} %all-gather.14.cloned.1.call-done, f32[3072]{0:T(1024)S(1)} %bitcast.37), kind=kOutput, calls=%fused_computation.5 | convolution fusion | flops 12894339072 | bytes 27275264 | tf_op jit(solution)/shard_map/dot_general | solution.py:33
  288.4 15.2 %all-gather.10.cloned.1.call-done = bf16[1,1024,1024]{2,1,0:T(8,128)(2,1)} async-done(((bf16[1,512,1024]{2,1,0:T(8,128)(2,1)}), bf16[1,1024,1024]{2,1,0:T(8,128)(2,1)}) %all-gather.10.cloned.1.call-update) | async-done | bytes 2097168 | tf_op jit(solution)/shard_map/all_gather | solution.py:55
  303.6 9.8 %fusion.1 = bf16[2048,1024]{1,0:T(8,128)(2,1)S(1)} fusion(f32[1024,2048]{0,1:T(8,128)} %fusion.3, bf16[2048,1024]{1,0:T(8,128)(2,1)} %bitcast, bf16[1,1024,1024]{2,1,0:T(8,128)(2,1)} %all-gather.10.cloned.1.call-done, f32[1024]{0:T(1024)S(1)} %bitcast.38), kind=kOutput, calls=%fused_computation.3 | convolution fusion | flops 4304404480 | bytes 18878464 | tf_op jit(solution)/shard_map/dot_general | solution.py:33
  313.4 3.2 copy.13
  316.6 97.4 %all_to_all.18 = bf16[1,4,512,1024]{3,1,0,2:T(4,128)(2,1)S(1)} all-to-all(bf16[1,4,512,1024]{3,1,0,2:T(4,128)(2,1)S(1)} %copy.13), channel_id=1, replica_groups=mesh['row'=2,'col'=4,'tm'=4] {'tm'}, dimensions={2} | all-to-all | bytes 8388608 | tf_op jit(solution)/shard_map/all_to_all | solution.py:68
  414.0 9.4 %convolution_bitcast_fusion = f32[4,4,128,1024]{3,0,2,1:T(4,128)S(1)} fusion(bf16[1,4,4,128,1024]{4,1,3,2,0:T(4,128)(2,1)S(1)} %bitcast.35, f32[4,4]{1,0:T(4,128)S(1)} %copy-done), kind=kOutput, calls=%fused_computation.7 | convolution fusion | flops 100663296 | bytes 12582976 | tf_op jit(solution)/shard_map/ft,tabc->fabc/dot_general | solution.py:65
  423.5 8.3 %copy.16 = f32[4,4,128,1024]{3,2,1,0:T(8,128)} copy(f32[4,4,128,1024]{3,0,2,1:T(4,128)S(1)} %convolution_bitcast_fusion) | data formatting | bytes 16777216 | tf_op jit(solution)/shard_map/ft,tabc->fabc/dot_general | solution.py:65
  (14 shorter events, 0.1 us)
Async XLA Ops:
  6.5 407.5 %copy-start = (f32[4,4]{1,0:T(4,128)S(1)}, f32[4,4]{1,0:T(4,128)}, u32[]{:S(2)}) copy-start(f32[4,4]{1,0:T(4,128)} %param.11) | copy-start | bytes 196
  6.5 127.4 %copy-start.2 = (bf16[768]{0:T(1024)(128)(2,1)S(1)}, bf16[768]{0:T(1024)(128)(2,1)}, u32[]{:S(2)}) copy-start(bf16[768]{0:T(1024)(128)(2,1)} %param.9) | copy-start | bytes 4612
  6.5 128.1 %copy-start.3 = (bf16[256]{0:T(256)(128)(2,1)S(1)}, bf16[256]{0:T(256)(128)(2,1)}, u32[]{:S(2)}) copy-start(bf16[256]{0:T(256)(128)(2,1)} %param.8) | copy-start | bytes 1540
  6.5 68.6 %all-gather.12.cloned.1.call-start = ((), (), s32[]{:S(2)}) async-start(), calls=%async_computation.3 | async-start | bytes 3932160 | tf_op jit(solution)/shard_map/all_gather | solution.py:47
  7.3 98.0 %all-gather.8.cloned.1.call-start = ((), (), s32[]{:S(2)}) async-start(), calls=%async_computation.1 | async-start | bytes 1310720 | tf_op jit(solution)/shard_map/all_gather | solution.py:46
  8.0 177.5 %all-gather.14.cloned.1.call-start = ((), (), s32[]{:S(2)}) async-start(), calls=%async_computation.4 | async-start | bytes 9437184 | tf_op jit(solution)/shard_map/all_gather | solution.py:55
  75.1 193.9 %all-gather.16.cloned.1.call-start = ((), (), s32[]{:S(2)}) async-start(), calls=%async_computation.5 | async-start | bytes 15728640 | tf_op jit(solution)/shard_map/all_gather | solution.py:53
  75.7 227.8 %all-gather.10.cloned.1.call-start = ((), (), s32[]{:S(2)}) async-start(), calls=%async_computation.2 | async-start | bytes 3145728 | tf_op jit(solution)/shard_map/all_gather | solution.py:55
  105.3 55.2 %copy-start.1 = (bf16[1,512,1024]{2,1,0:T(8,128)(2,1)S(1)}, bf16[1,512,1024]{2,1,0:T(8,128)(2,1)}, u32[]{:S(2)}) copy-start(bf16[1,512,1024]{2,1,0:T(8,128)(2,1)} %all-gather.8.cloned.1.call-done) | copy-start | bytes 3145732
  105.3 14.4 %collective-permute-start = (bf16[1,512,1024]{2,1,0:T(8,128)(2,1)}, bf16[1,512,1024]{2,1,0:T(8,128)(2,1)S(1)}, u32[]{:S(2)}, u32[]{:S(2)}) collective-permute-start(bf16[1,512,1024]{2,1,0:T(8,128)(2,1)} %all-gather.8.cloned.1.call-done), channel_id=1, source_target_pairs={{0,4},{4,8},{8,12},{12,0},{1,5},{5,9},{9,13},{13,1},{2,6},{6,10},{... | collective-permute-start | bytes 3145736 | tf_op jit(solution)/shard_map/ppermute | solution.py:19
  119.7 14.2 %collective-permute-start.1 = (bf16[1,512,1024]{2,1,0:T(8,128)(2,1)S(1)}, bf16[1,512,1024]{2,1,0:T(8,128)(2,1)S(1)}, u32[]{:S(2)}, u32[]{:S(2)}) collective-permute-start(bf16[1,512,1024]{2,1,0:T(8,128)(2,1)S(1)} %collective-permute-done), channel_id=1, source_target_pairs={{0,4},{4,8},{8,12},{12,0},{1,5},{5,9},{9,13},{13,1},{2,6},{6,10},{... | collective-permute-start | bytes 3145736 | tf_op jit(solution)/shard_map/ppermute | solution.py:19
  133.9 29.7 %collective-permute-start.2 = (bf16[1,512,1024]{2,1,0:T(8,128)(2,1)S(1)}, bf16[1,512,1024]{2,1,0:T(8,128)(2,1)}, u32[]{:S(2)}, u32[]{:S(2)}) collective-permute-start(bf16[1,512,1024]{2,1,0:T(8,128)(2,1)S(1)} %collective-permute-done.1), channel_id=1, source_target_pairs={{0,4},{4,8},{8,12},{12,0},{1,5},{5,9},{9,13},{13,1},{2,6},{6,10},{... | collective-permute-start | bytes 3145736 | tf_op jit(solution)/shard_map/ppermute | solution.py:19
Sparse Core Ops, SparseCore 0:
  8.9 66.1 all-gather.11
  76.7 28.5 all-gather.7
  106.8 78.6 all-gather.13
  186.9 82.0 all-gather.15
  270.4 33.0 all-gather.9
